TPU v7x, 32 devices: a whole 2x2x4 slice. The times are simulated.
32 devices in a mesh: group: 2 (over y), patch: 4 (over z), head: 2 (over x), cfg: 2 (over core).
Axes of the slice: x: 2, y: 2, z: 4, core: 2. Of those that a mesh axis runs over, the one named last changes fastest.
Arguments:
- fresh_query: bfloat16 [4, 256, 2560], P(('group', 'cfg'), ('patch', 'head')), parts along dimension 0, may hold values from -32 to 32
- fresh_key: bfloat16 [4, 256, 2560], P(('group', 'cfg'), ('patch', 'head')), parts along dimension 0, may hold values from -9 to 9
- fresh_value: bfloat16 [4, 256, 2560], P(('group', 'cfg'), ('patch', 'head')), parts along dimension 0, may hold values from -12 to 12
- stale_key: bfloat16 [4, 256, 2560], P(('group', 'cfg'), 'patch', 'head'), parts along dimension 0, may hold values from -8 to 8
- stale_value: bfloat16 [4, 256, 2560], P(('group', 'cfg'), 'patch', 'head'), parts along dimension 0, may hold values from -12 to 12
- cross_query: bfloat16 [4, 256, 2560], P(('group', 'cfg'), ('patch', 'head')), parts along dimension 0, may hold values from -32 to 32
- text_key: bfloat16 [4, 512, 2560], P(('group', 'cfg'), None, 'head'), parts along dimension 0, may hold values from -8 to 8
- text_value: bfloat16 [4, 512, 2560], P(('group', 'cfg'), None, 'head'), parts along dimension 0, may hold values from -12 to 12
- text_mask: int32 [4, 512], P(('group', 'cfg')), parts along dimension 0, may hold values from 0 to 1, as said below
Outputs:
- self_mixed: bfloat16 [4, 256, 2560], P(('group', 'cfg'), ('patch', 'head')), parts along dimension 0
- cross_mixed: bfloat16 [4, 256, 2560], P(('group', 'cfg'), ('patch', 'head')), parts along dimension 0
There are 2 independent parts, one for each index of `group`. A program takes and returns all parts, laid end to end along the dimension named above; each array names one. Nothing has to cross between parts.
Inputs may be any that keep to these rules, and one draw needn't show every extreme that they name: In each branch the ones of text_mask form a prefix of 32 or more positions; in one of the two branches all 512 are ones, in the other some are zeros.
All inputs are finite; a program needn't handle non-finite values.
Results may differ from a plain program's by a relative error of at most 0.005.
Values may be sent and summed in bfloat16 or wider, within the bound.
A program may use at most 128 MiB of HBM per device.

v0:
```python
import math
import jax
import jax.numpy as jnp
from jax import lax
from jax.sharding import PartitionSpec as P

HD = 128


def scaled_scores(queries, key_block):
    return jnp.einsum("qhd,khd->qhk", queries, key_block, preferred_element_type=jnp.float32) * (
        1.0 / math.sqrt(HD)
    )


def absorb(running, scores, value_block, keeper):
    run_top, run_total, run_sum = running
    if keeper is None:
        piece_top = jnp.max(scores, axis=-1, keepdims=True)
        new_top = piece_top
        weights = jnp.exp(scores - new_top)
    else:
        piece_top = jnp.max(jnp.where(keeper, scores, -jnp.inf), axis=-1, keepdims=True)
        new_top = jnp.maximum(run_top, piece_top)
        weights = jnp.where(keeper, jnp.exp(jnp.where(keeper, scores, new_top) - new_top), 0.0)
    factor = jnp.exp(run_top - new_top)
    run_total = run_total * factor + jnp.sum(weights, axis=-1, keepdims=True)
    run_sum = run_sum * factor + jnp.einsum(
        "qhk,khd->qhd",
        weights.astype(jnp.bfloat16),
        value_block,
        preferred_element_type=jnp.float32,
    )
    return (new_top, run_total, run_sum)


def masked_mix(queries, key_block, value_block, usable):
    scores = scaled_scores(queries, key_block)
    row_top = jnp.max(jnp.where(usable, scores, -jnp.inf), axis=-1, keepdims=True)
    weights = jnp.where(usable, jnp.exp(jnp.where(usable, scores, row_top) - row_top), 0.0)
    totals = jnp.sum(weights, axis=-1, keepdims=True)
    mixture = jnp.einsum(
        "qhk,khd->qhd",
        weights.astype(jnp.bfloat16),
        value_block,
        preferred_element_type=jnp.float32,
    )
    return mixture / totals


def per_device(
    fresh_query,
    fresh_key,
    fresh_value,
    stale_key,
    stale_value,
    cross_query,
    text_key,
    text_value,
    text_mask,
):
    usable = (text_mask[0] > 0)[None, None, :]
    text_rows = text_key.shape[1]
    token_rows = fresh_query.shape[1]
    local_query, local_key, local_value = (
        lax.all_to_all(fresh_query, "head", split_axis=2, concat_axis=1, tiled=True),
        lax.all_to_all(fresh_key, "head", split_axis=2, concat_axis=1, tiled=True),
        lax.all_to_all(fresh_value, "head", split_axis=2, concat_axis=1, tiled=True),
    )
    patch_rows = local_query.shape[1]
    heads_here = local_query.shape[2] // HD
    queries = local_query.reshape(patch_rows, heads_here, HD)
    own_keys = local_key.reshape(patch_rows, heads_here, HD)
    own_values = local_value.reshape(patch_rows, heads_here, HD)
    own_first = lax.axis_index("patch") * patch_rows
    starting = (
        jnp.full((patch_rows, heads_here, 1), -jnp.inf, jnp.float32),
        jnp.zeros((patch_rows, heads_here, 1), jnp.float32),
        jnp.zeros((patch_rows, heads_here, HD), jnp.float32),
    )
    opening = absorb(starting, scaled_scores(queries, own_keys), own_values, None)
    piece_key = lax.all_gather(stale_key, "patch", axis=1, tiled=True)
    piece_value = lax.all_gather(stale_value, "patch", axis=1, tiled=True)
    row_count = piece_key.shape[1]
    keys_here = piece_key.reshape(row_count, heads_here, HD)
    values_here = piece_value.reshape(row_count, heads_here, HD)
    positions = jnp.arange(row_count, dtype=jnp.int32)
    keeper = ((positions < own_first) | (positions >= own_first + patch_rows))[None, None, :]
    run_top, run_total, run_sum = absorb(
        opening, scaled_scores(queries, keys_here), values_here, keeper
    )
    self_block = (run_sum / run_total).reshape(1, patch_rows, heads_here * HD).astype(jnp.bfloat16)
    all_heads = cross_query.shape[2] // HD
    cross_heads = cross_query.reshape(token_rows, all_heads, HD)
    piece_key, piece_value = lax.all_gather(
        (
            text_key.reshape(1, text_rows, heads_here, HD),
            text_value.reshape(1, text_rows, heads_here, HD),
        ),
        "head",
        axis=2,
        tiled=True,
    )
    mixture = masked_mix(cross_heads, piece_key[0], piece_value[0], usable)
    gathered = mixture.astype(jnp.bfloat16)[None]
    cross_block = gathered.reshape(1, token_rows, all_heads * HD)
    self_mixed = lax.all_to_all(self_block, "head", split_axis=1, concat_axis=2, tiled=True)
    return (self_mixed, cross_block)


def solution(mesh):
    return jax.shard_map(
        per_device,
        mesh=mesh,
        in_specs=(
            P(("group", "cfg"), ("patch", "head"), None),
            P(("group", "cfg"), ("patch", "head"), None),
            P(("group", "cfg"), ("patch", "head"), None),
            P(("group", "cfg"), "patch", "head"),
            P(("group", "cfg"), "patch", "head"),
            P(("group", "cfg"), ("patch", "head"), None),
            P(("group", "cfg"), None, "head"),
            P(("group", "cfg"), None, "head"),
            P(("group", "cfg"), None),
        ),
        out_specs=(
            P(("group", "cfg"), ("patch", "head"), None),
            P(("group", "cfg"), ("patch", "head"), None),
        ),
        check_vma=False,
    )
```

profile of v0, /device:TPU:0, one launch (start us, length us, event | category | flops | bytes accessed | tf_op | source)
XLA Modules:
  0.0 149.4 jit_solution(1958415783337173645)
XLA Ops:
  7.2 0.0 all-gather.3.cloned.1.call-start
  7.2 1.6 %copy.97 = bf16[1,512,1280]{1,2,0:T(8,128)(2,1)S(1)} copy(bf16[1,512,1280]{2,1,0:T(8,128)(2,1)} %param.15) | data formatting | bytes 2621440 | tf_op args[6]
  8.8 1.5 copy.98
  10.3 0.0 all-gather.3.cloned.1.call-update
  10.3 0.9 copy-done.5
  11.2 0.9 copy.79
  12.1 0.6 broadcast.39
  12.7 14.4 %reduce.2 = bf16[2560,32]{1,0:T(8,128)(2,1)S(1)} reduce(bf16[2560,1,32]{2,1,0:T(2,128)(2,1)S(1)} %bitcast.72, bf16[]{:T(256)} %broadcast.39), dimensions={1}, to_apply=%bitcast.62.reduce_sub_computation | reduce | bytes 327682
  27.1 1.3 reshape.109
  28.4 4.2 %all-to-all-start.1 = ((bf16[2,2,20480]{2,1,0:T(2,128)(2,1)}), bf16[2,2,20480]{2,1,0:T(2,128)(2,1)S(1)}, u32[]{:S(2)}, u32[]{:S(2)}) async-start(bf16[2,2,20480]{2,1,0:T(2,128)(2,1)} %reshape.109), calls=%async_computation.1 | async-start | bytes 327680 | tf_op jit(solution)/shard_map/all_to_all | solution.py:66
  32.7 0.6 copy.100
  33.3 1.4 copy.101
  34.8 0.0 all-gather.5.cloned.1.call-update
  34.8 0.9 copy-done.3
  35.7 19.2 %all_gather.12 = bf16[1,256,1280]{2,1,0:T(8,128)(2,1)S(1)} all-gather(bf16[1,64,1280]{2,1,0:T(8,128)(2,1)S(1)} %copy-done.3), channel_id=1, replica_groups=mesh['group'=2,'patch'=4,'head'=2,'cfg'=2] {'patch'}, dimensions={1}, use_global_device_ids=true | all-gather | bytes 819200 | tf_op jit(solution)/shard_map/all_gather | solution.py:82
  54.8 0.9 copy.76
  55.8 0.0 copy-start.4
  55.8 14.3 %reduce.3 = bf16[2560,32]{1,0:T(8,128)(2,1)S(1)} reduce(bf16[2560,1,32]{2,1,0:T(2,128)(2,1)S(1)} %bitcast.78, bf16[]{:T(256)} %broadcast.39), dimensions={1}, to_apply=%bitcast.60.reduce_sub_computation | reduce | bytes 327682
  70.1 0.0 copy-start.2
  70.1 1.3 reshape.107
  71.4 0.0 all-to-all-done.1
  71.4 4.1 %all-to-all-start = ((bf16[2,2,20480]{2,1,0:T(2,128)(2,1)}), bf16[2,2,20480]{2,1,0:T(2,128)(2,1)}, u32[]{:S(2)}, u32[]{:S(2)}) async-start(bf16[2,2,20480]{2,1,0:T(2,128)(2,1)} %reshape.107), calls=%async_computation | async-start | bytes 327680 | tf_op jit(solution)/shard_map/all_to_all | solution.py:67
  75.5 16.1 %all_gather.13 = bf16[1,256,1280]{2,1,0:T(8,128)(2,1)S(1)} all-gather(bf16[1,64,1280]{2,1,0:T(8,128)(2,1)S(1)} %copy-done.4), channel_id=1, replica_groups=mesh['group'=2,'patch'=4,'head'=2,'cfg'=2] {'patch'}, dimensions={1}, use_global_device_ids=true | all-gather | bytes 819200 | tf_op jit(solution)/shard_map/all_gather | solution.py:83
  91.6 0.1 reshape.104
  91.7 0.2 copy.89
  92.0 0.0 copy-start.7
  92.0 0.2 copy.92
  92.2 0.7 copy-done.7
  92.9 0.9 copy.84
  93.8 14.3 %reduce.4 = bf16[2560,32]{1,0:T(8,128)(2,1)S(1)} reduce(bf16[2560,1,32]{2,1,0:T(2,128)(2,1)S(1)} %bitcast.79, bf16[]{:T(256)} %broadcast.39), dimensions={1}, to_apply=%bitcast.64.reduce_sub_computation | reduce | bytes 327682
  108.1 1.3 reshape.111
  109.4 0.0 all-to-all-done
  109.4 4.3 %all-to-all-start.2 = ((bf16[2,2,20480]{2,1,0:T(2,128)(2,1)}), bf16[2,2,20480]{2,1,0:T(2,128)(2,1)}, u32[]{:S(2)}, u32[]{:S(2)}) async-start(bf16[2,2,20480]{2,1,0:T(2,128)(2,1)} %reshape.111), calls=%async_computation.2 | async-start | bytes 327680 | tf_op jit(solution)/shard_map/all_to_all | solution.py:68
  113.8 1.5 reshape.110
  115.2 0.7 copy.80
  116.0 0.1 reshape.99
  116.2 1.5 reshape.108
  117.6 0.7 copy.77
  118.4 0.1 reshape.98
  118.5 0.0 all-to-all-done.2
  118.6 1.5 reshape.112
  120.1 1.7 %copy.85 = bf16[1,32,2560]{2,1,0:T(8,128)(2,1)} copy(bf16[1,32,2560]{1,0,2:T(2,128)(2,1)S(1)} %bitcast.75) | data formatting | bytes 327680 | tf_op jit(solution)/shard_map/all_to_all | solution.py:68
  121.8 1.0 all_to_all.53
  122.8 0.1 reshape.100
  122.9 0.2 fusion.49
  123.1 0.3 select_reduce_fusion.1
  123.5 0.1 fusion.38
  123.6 0.3 fusion.32
  123.9 0.3 fusion.17
  124.2 0.4 fusion.22
  124.6 0.1 copy.94
  124.8 0.1 convert_element_type.32
  124.9 1.6 %reduce.5 = bf16[64,1280]{1,0:T(8,128)(2,1)S(1)} reduce(bf16[64,1,1280]{2,1,0:T(2,128)(2,1)S(1)} %bitcast.81, bf16[]{:T(256)} %broadcast.39), dimensions={1}, to_apply=%bitcast.66.reduce_sub_computation | reduce | bytes 327682
  126.5 0.7 reshape.113
  127.2 3.4 %all-to-all-start.3 = ((bf16[2,2,20480]{2,1,0:T(2,128)(2,1)}), bf16[2,2,20480]{2,1,0:T(2,128)(2,1)S(1)}, u32[]{:S(2)}, u32[]{:S(2)}) async-start(bf16[2,2,20480]{2,1,0:T(2,128)(2,1)} %reshape.113), calls=%async_computation.3 | async-start | bytes 327680 | tf_op jit(solution)/shard_map/all_to_all | solution.py:107
  130.7 4.6 %all-to-all-done.3 = bf16[2,2,20480]{2,1,0:T(2,128)(2,1)S(1)} async-done(((bf16[2,2,20480]{2,1,0:T(2,128)(2,1)}), bf16[2,2,20480]{2,1,0:T(2,128)(2,1)S(1)}, u32[]{:S(2)}, u32[]{:S(2)}) %all-to-all-start.3) | async-done | bytes 163872 | tf_op jit(solution)/shard_map/all_to_all | solution.py:107
  135.3 0.2 reshape.114
  135.4 0.7 copy.107
  136.1 2.8 %select_reduce_fusion = (f32[32,20]{0,1:T(8,128)S(1)}, f32[32,20,512]{2,0,1:T(8,128)S(1)}) fusion(pred[512]{0:T(512)(128)(4,1)S(1)} %compare_reduce_fusion, bf16[32,20,128]{2,1,0:T(8,128)(2,1)S(1)} %reshape.104, bf16[1,512,20,128]{3,1,0,2:T(8,128)(2,1)} %all-gather.3.cloned.1.call-done), kind=kOutput, calls=%fused_computation.7 | convolution fusion | flops 84868480 | bytes 4099072 | tf_op jit(solution)/shard_map/qhd,khd->qhk/dot_general | solution.py:11
  138.9 0.4 fusion.26
  139.4 0.0 all-gather.5.cloned.1.call-done
  139.4 2.3 %fusion.23 = bf16[32,20,128]{2,0,1:T(8,128)(2,1)S(1)} fusion(bf16[1,512,20,128]{3,1,0,2:T(8,128)(2,1)} %all-gather.5.cloned.1.call-done, f32[32,20,512]{2,0,1:T(8,128)S(1)} %get-tuple-element.10, f32[32,20]{0,1:T(8,128)S(1)} %get-tuple-element.9, pred[512]{0:T(512)(128)(4,1)S(1)} %compare_reduce_fusion, f32[32,20]{0,1:T(8,128)S(1)} %fusion.26), kind=kOutput, calls=%fused_computation.21 | convolution fusion | flops 85360640 | bytes 4101632 | tf_op jit(solution)/shard_map/qhk,khd->qhd/dot_general | solution.py:42
  141.7 0.1 copy.102
  141.8 0.8 reshape_broadcast_in_dim.3
  (24 shorter events, 0.2 us)
Async XLA Ops:
  7.2 129.0 %all-gather.3.cloned.1.call-start = ((), (), s32[]{:S(2)}) async-start(), calls=%async_computation.4 | async-start | bytes 3932160 | tf_op jit(solution)/shard_map/all_gather | solution.py:95
  10.3 0.9 copy-start.5
  12.7 20.0 %copy-start = (bf16[1,512,1280]{2,1,0:T(8,128)(2,1)S(1)}, bf16[1,512,1280]{2,1,0:T(8,128)(2,1)}, u32[]{:S(2)}) copy-start(bf16[1,512,1280]{2,1,0:T(8,128)(2,1)} %param.16) | copy-start | bytes 3932164
  28.4 43.0 %all-to-all-start.1 = ((bf16[2,2,20480]{2,1,0:T(2,128)(2,1)}), bf16[2,2,20480]{2,1,0:T(2,128)(2,1)S(1)}, u32[]{:S(2)}, u32[]{:S(2)}) async-start(bf16[2,2,20480]{2,1,0:T(2,128)(2,1)} %reshape.109), calls=%async_computation.1 | async-start | bytes 327680 | tf_op jit(solution)/shard_map/all_to_all | solution.py:66
  32.7 106.7 %all-gather.5.cloned.1.call-start = ((), (), s32[]{:S(2)}) async-start(), calls=%async_computation.5 | async-start | bytes 3932160 | tf_op jit(solution)/shard_map/all_gather | solution.py:95
  34.8 0.9 copy-start.3
  34.8 20.1 %copy-start.6 = (bf16[1,32,2560]{2,1,0:T(8,128)(2,1)S(1)}, bf16[1,32,2560]{2,1,0:T(8,128)(2,1)}, u32[]{:S(2)}) copy-start(bf16[1,32,2560]{2,1,0:T(8,128)(2,1)} %param.10) | copy-start | bytes 491524
  55.8 19.7 %copy-start.4 = (bf16[1,64,1280]{2,1,0:T(8,128)(2,1)S(1)}, bf16[1,64,1280]{2,1,0:T(8,128)(2,1)}, u32[]{:S(2)}) copy-start(bf16[1,64,1280]{2,1,0:T(8,128)(2,1)} %param.13) | copy-start | bytes 491524
  70.1 21.5 %copy-start.2 = (bf16[1,32,2560]{2,1,0:T(8,128)(2,1)S(1)}, bf16[1,32,2560]{2,1,0:T(8,128)(2,1)}, u32[]{:S(2)}) copy-start(bf16[1,32,2560]{2,1,0:T(8,128)(2,1)} %param.14) | copy-start | bytes 491524
  71.4 20.3 %copy-start.1 = (bf16[2,2,20480]{2,1,0:T(2,128)(2,1)}, bf16[2,2,20480]{2,1,0:T(2,128)(2,1)S(1)}, u32[]{:S(2)}) copy-start(bf16[2,2,20480]{2,1,0:T(2,128)(2,1)S(1)} %all-to-all-done.1) | copy-start | bytes 491524
  71.4 38.0 %all-to-all-start = ((bf16[2,2,20480]{2,1,0:T(2,128)(2,1)}), bf16[2,2,20480]{2,1,0:T(2,128)(2,1)}, u32[]{:S(2)}, u32[]{:S(2)}) async-start(bf16[2,2,20480]{2,1,0:T(2,128)(2,1)} %reshape.107), calls=%async_computation | async-start | bytes 327680 | tf_op jit(solution)/shard_map/all_to_all | solution.py:67
  92.0 0.9 copy-start.7
  109.4 9.1 %all-to-all-start.2 = ((bf16[2,2,20480]{2,1,0:T(2,128)(2,1)}), bf16[2,2,20480]{2,1,0:T(2,128)(2,1)}, u32[]{:S(2)}, u32[]{:S(2)}) async-start(bf16[2,2,20480]{2,1,0:T(2,128)(2,1)} %reshape.111), calls=%async_computation.2 | async-start | bytes 327680 | tf_op jit(solution)/shard_map/all_to_all | solution.py:68
  124.6 6.0 %copy-start.8 = (s32[1,512]{1,0:T(1,128)S(1)}, s32[1,512]{1,0:T(1,128)}, u32[]{:S(2)}) copy-start(s32[1,512]{1,0:T(1,128)} %param.17) | copy-start | bytes 6148
  127.2 8.1 %all-to-all-start.3 = ((bf16[2,2,20480]{2,1,0:T(2,128)(2,1)}), bf16[2,2,20480]{2,1,0:T(2,128)(2,1)S(1)}, u32[]{:S(2)}, u32[]{:S(2)}) async-start(bf16[2,2,20480]{2,1,0:T(2,128)(2,1)} %reshape.113), calls=%async_computation.3 | async-start | bytes 327680 | tf_op jit(solution)/shard_map/all_to_all | solution.py:107
Sparse Core Ops, SparseCore 0:
  10.4 43.4 all-gather.2
  55.5 40.7 all-gather.4
where the time goes:
time: 150 us; the launch traced here: 149 us
  other arithmetic  45.5 us (30%)
  blocking collectives  35.3 us (24%)
  local copies, waits for them, and re-layouts  27.1 us (18%)
  starting transfers between devices  16 us (11%)
  between operations  14.4 us (10%)
  matrix products  6.43 us (4%)
  waiting for transfers between devices  4.66 us (3%)
    unnamed x4, other arithmetic  44.7 us
    all_gather x1, blocking collectives, per_device(): piece_key = lax.all_gather(stale_key, 'patch', axis=1, tiled=True)  19.2 us
    unnamed x33, local copies, waits for them, and re-layouts  17.3 us
    all_gather x1, blocking collectives, per_device(): piece_value = lax.all_gather(stale_value, 'patch', axis=1, tiled=True)  16.1 us
    all_to_all x1, waiting for transfers between devices, per_device(): lax.all_to_all(self_block, 'head', split_axis=1, concat_axis=2, tiled=True)  4.6 us
    all_to_all x1, starting transfers between devices, per_device(): lax.all_to_all(fresh_value, 'head', split_axis=2, concat_axis=1, tiled=True)  4.28 us
    all_to_all x1, starting transfers between devices, per_device(): lax.all_to_all(fresh_query, 'head', split_axis=2, concat_axis=1, tiled=True)  4.23 us
    all_to_all x1, starting transfers between devices, per_device(): lax.all_to_all(fresh_key, 'head', split_axis=2, concat_axis=1, tiled=True)  4.05 us
  transfers between devices with their start and end apart: 6, of which 1 were waited for; matrix products, arithmetic and copies ran while one was open for 46% of the time, Pallas kernels for 0%

commit v1 on v0

--- a/solution.py
+++ b/solution.py
@@ -5,6 +5,17 @@
 from jax.sharding import PartitionSpec as P
 
 HD = 128
+
+
+def _rest_sites(u, dimension_no):
+    u = jnp.moveaxis(u, 0, dimension_no)
+    work_now = u.shape
+    spare = u.reshape(
+        *work_now[:dimension_no],
+        work_now[dimension_no] * work_now[dimension_no + 1],
+        *work_now[dimension_no + 2 :]
+    )
+    return spare
 
 
 def scaled_scores(queries, key_block):
@@ -80,7 +91,23 @@
     )
     opening = absorb(starting, scaled_scores(queries, own_keys), own_values, None)
     piece_key = lax.all_gather(stale_key, "patch", axis=1, tiled=True)
-    piece_value = lax.all_gather(stale_value, "patch", axis=1, tiled=True)
+    n_parts = jax.lax.psum(1, "patch")
+    buffer = [(kk, (kk + 1) % n_parts) for kk in range(n_parts)]
+    tray = [(b, idx) for idx, b in buffer]
+    n_now, mid_arr = ([], [])
+    dev_j = 0
+    while dev_j < n_parts - 1:
+        if dev_j % 2 == 0:
+            block_next = jax.lax.ppermute(n_now[-1] if n_now else stale_value, "patch", buffer)
+            n_now.append(block_next)
+        else:
+            mid_arr.append(jax.lax.ppermute(mid_arr[-1] if mid_arr else stale_value, "patch", tray))
+        dev_j = dev_j + 1
+    top = jnp.stack([*n_now[::-1], stale_value, *mid_arr], axis=0)
+    shaped = jax.lax.axis_index("patch")
+    now = shaped - len(n_now)
+    top = top[(jnp.arange(n_parts) - now) % n_parts]
+    piece_value = _rest_sites(top, 1)
     row_count = piece_key.shape[1]
     keys_here = piece_key.reshape(row_count, heads_here, HD)
     values_here = piece_value.reshape(row_count, heads_here, HD)

time: 150 us -> 144 us (0.960)
  blocking collectives: 35.3 us -> 16.6 us
  waiting for transfers between devices: 4.66 us -> 17.6 us
  local copies, waits for them, and re-layouts: 27.1 us -> 22 us
  starting transfers between devices: 16 us -> 19.3 us
    all_gather x1 -> x0, blocking collectives: 16.1 us -> none  [per_device(): piece_value = lax.all_gather(stale_value, 'patch', axis=1, tiled=True)]
    ppermute x0 -> x3, waiting for transfers between devices: none -> 6.98 us  [the longest x2 6.98 us: per_device(): jax.lax.ppermute(n_now[-1] if n_now else stale_value, 'patch', buffer)]
    ppermute x0 -> x3, starting transfers between devices: none -> 5.26 us  [the longest x2 3.16 us: per_device(): jax.lax.ppermute(n_now[-1] if n_now else stale_value, 'patch', buffer)]
    all_to_all x1, waiting for transfers between devices: 0.01 us -> 4.62 us  [per_device(): lax.all_to_all(fresh_key, 'head', split_axis=2, concat_axis=1, tiled=True)]
    unnamed x33, local copies, waits for them, and re-layouts: 17.3 us -> 13.4 us
    all_gather x1, blocking collectives: 19.2 us -> 16.6 us  [per_device(): piece_key = lax.all_gather(stale_key, 'patch', axis=1, tiled=True)]
    all_to_all x3, local copies, waits for them, and re-layouts: 2.72 us -> 0.77 us  [per_device(): lax.all_to_all(fresh_value, 'head', split_axis=2, concat_axis=1, tiled=True)]
  transfers between devices with their start and end apart: 6 -> 9, of which waited for: 1 -> 4; matrix products, arithmetic and copies ran while one was open for 46% -> 47% of each run, Pallas kernels for 0% -> 0%
where the time goes in v1:
time: 144 us; the launch traced here: 143 us
  other arithmetic  46.7 us (32%)
  local copies, waits for them, and re-layouts  22 us (15%)
  starting transfers between devices  19.3 us (13%)
  waiting for transfers between devices  17.6 us (12%)
  blocking collectives  16.6 us (12%)
  between operations  14.5 us (10%)
  matrix products  6.39 us (4%)
    unnamed x4, other arithmetic  44.7 us
    all_gather x1, blocking collectives, per_device(): piece_key = lax.all_gather(stale_key, 'patch', axis=1, tiled=True)  16.6 us
    unnamed x33, local copies, waits for them, and re-layouts  13.4 us
    ppermute x2, waiting for transfers between devices, per_device(): jax.lax.ppermute(n_now[-1] if n_now else stale_value, 'patch', buffer)  6.98 us
    all_to_all x1, waiting for transfers between devices, per_device(): lax.all_to_all(fresh_key, 'head', split_axis=2, concat_axis=1, tiled=True)  4.62 us
    all_to_all x1, waiting for transfers between devices, per_device(): lax.all_to_all(self_block, 'head', split_axis=1, concat_axis=2, tiled=True)  4.6 us
    all_to_all x1, starting transfers between devices, per_device(): lax.all_to_all(fresh_value, 'head', split_axis=2, concat_axis=1, tiled=True)  3.65 us
    all_to_all x1, starting transfers between devices, per_device(): lax.all_to_all(fresh_key, 'head', split_axis=2, concat_axis=1, tiled=True)  3.44 us
  transfers between devices with their start and end apart: 9, of which 4 were waited for; matrix products, arithmetic and copies ran while one was open for 47% of the time, Pallas kernels for 0%

profile of v1, /device:TPU:0, one launch (start us, length us, event | category | flops | bytes accessed | tf_op | source)
XLA Modules:
  0.0 143.1 jit_solution(11603193958656270131)
XLA Ops:
  7.2 0.0 all-gather.3.cloned.1.call-start
  7.2 1.6 %copy.94 = bf16[1,512,1280]{1,2,0:T(8,128)(2,1)S(1)} copy(bf16[1,512,1280]{2,1,0:T(8,128)(2,1)} %param.15) | data formatting | bytes 2621440 | tf_op args[6]
  8.8 1.5 %copy.95 = bf16[1,512,10,128]{3,1,0,2:T(8,128)(2,1)} copy(bf16[1,512,10,128]{1,3,2,0:T(8,128)(2,1)S(1)} %bitcast.82) | data formatting | bytes 2621440 | tf_op jit(solution)/shard_map/reshape | solution.py:124
  10.3 0.0 all-gather.3.cloned.1.call-update
  10.3 3.1 %collective-permute-start = (bf16[1,64,1280]{2,1,0:T(8,128)(2,1)}, bf16[1,64,1280]{2,1,0:T(8,128)(2,1)}, u32[]{:S(2)}, u32[]{:S(2)}) collective-permute-start(bf16[1,64,1280]{2,1,0:T(8,128)(2,1)} %param.13), channel_id=1, source_target_pairs={{0,4},{4,8},{8,12},{12,0},{1,5},{5,9},{9,13},{13,1},{2,6},{6,10},{... | collective-permute-start | bytes 491528 | tf_op jit(solution)/shard_map/ppermute | solution.py:101
  13.4 2.1 %collective-permute-start.2 = (bf16[1,64,1280]{2,1,0:T(8,128)(2,1)}, bf16[1,64,1280]{2,1,0:T(8,128)(2,1)}, u32[]{:S(2)}, u32[]{:S(2)}) collective-permute-start(bf16[1,64,1280]{2,1,0:T(8,128)(2,1)} %param.13), channel_id=1, source_target_pairs={{4,0},{8,4},{12,8},{0,12},{5,1},{9,5},{13,9},{1,13},{6,2},{10,6},{... | collective-permute-start | bytes 491528 | tf_op jit(solution)/shard_map/ppermute | solution.py:104
  15.5 0.9 copy.77
  16.4 0.6 broadcast.108
  17.0 14.4 %reduce.2 = bf16[2560,32]{1,0:T(8,128)(2,1)S(1)} reduce(bf16[2560,1,32]{2,1,0:T(2,128)(2,1)S(1)} %bitcast.78, bf16[]{:T(256)} %broadcast.108), dimensions={1}, to_apply=%bitcast.69.reduce_sub_computation | reduce | bytes 327682
  31.4 1.3 reshape.165
  32.7 3.4 %all-to-all-start.1 = ((bf16[2,2,20480]{2,1,0:T(2,128)(2,1)}), bf16[2,2,20480]{2,1,0:T(2,128)(2,1)S(1)}, u32[]{:S(2)}, u32[]{:S(2)}) async-start(bf16[2,2,20480]{2,1,0:T(2,128)(2,1)} %reshape.165), calls=%async_computation.1 | async-start | bytes 327680 | tf_op jit(solution)/shard_map/all_to_all | solution.py:77
  36.2 0.0 all-gather.5.cloned.1.call-start
  36.2 0.7 copy.97
  36.9 1.4 %copy.98 = bf16[1,512,10,128]{3,1,0,2:T(8,128)(2,1)} copy(bf16[1,512,10,128]{1,3,2,0:T(8,128)(2,1)S(1)} %bitcast.83) | data formatting | bytes 2621440 | tf_op jit(solution)/shard_map/reshape | solution.py:125
  38.3 0.0 all-gather.5.cloned.1.call-update
  38.4 0.9 copy-done.1
  39.2 0.1 reshape.149
  39.4 16.6 %all_gather.9 = bf16[1,256,1280]{2,1,0:T(8,128)(2,1)S(1)} all-gather(bf16[1,64,1280]{2,1,0:T(8,128)(2,1)S(1)} %copy-done.2), channel_id=1, replica_groups=mesh['group'=2,'patch'=4,'head'=2,'cfg'=2] {'patch'}, dimensions={1}, use_global_device_ids=true | all-gather | bytes 819200 | tf_op jit(solution)/shard_map/all_gather | solution.py:93
  56.0 0.2 copy.87
  56.3 0.9 copy.74
  57.2 14.3 %reduce.3 = bf16[2560,32]{1,0:T(8,128)(2,1)S(1)} reduce(bf16[2560,1,32]{2,1,0:T(2,128)(2,1)S(1)} %bitcast.84, bf16[]{:T(256)} %broadcast.108), dimensions={1}, to_apply=%bitcast.67.reduce_sub_computation | reduce | bytes 327682
  71.6 1.3 reshape.163
  72.9 0.9 copy.82
  73.8 14.3 %reduce.4 = bf16[2560,32]{1,0:T(8,128)(2,1)S(1)} reduce(bf16[2560,1,32]{2,1,0:T(2,128)(2,1)S(1)} %bitcast.85, bf16[]{:T(256)} %broadcast.108), dimensions={1}, to_apply=%bitcast.71.reduce_sub_computation | reduce | bytes 327682
  88.1 1.3 reshape.167
  89.4 3.4 %all-to-all-start = ((bf16[2,2,20480]{2,1,0:T(2,128)(2,1)}), bf16[2,2,20480]{2,1,0:T(2,128)(2,1)S(1)}, u32[]{:S(2)}, u32[]{:S(2)}) async-start(bf16[2,2,20480]{2,1,0:T(2,128)(2,1)} %reshape.163), calls=%async_computation | async-start | bytes 327680 | tf_op jit(solution)/shard_map/all_to_all | solution.py:78
  92.9 4.6 %all-to-all-done = bf16[2,2,20480]{2,1,0:T(2,128)(2,1)S(1)} async-done(((bf16[2,2,20480]{2,1,0:T(2,128)(2,1)}), bf16[2,2,20480]{2,1,0:T(2,128)(2,1)S(1)}, u32[]{:S(2)}, u32[]{:S(2)}) %all-to-all-start) | async-done | bytes 163872 | tf_op jit(solution)/shard_map/all_to_all | solution.py:78
  97.5 3.6 %all-to-all-start.2 = ((bf16[2,2,20480]{2,1,0:T(2,128)(2,1)}), bf16[2,2,20480]{2,1,0:T(2,128)(2,1)S(1)}, u32[]{:S(2)}, u32[]{:S(2)}) async-start(bf16[2,2,20480]{2,1,0:T(2,128)(2,1)} %reshape.167), calls=%async_computation.2 | async-start | bytes 327680 | tf_op jit(solution)/shard_map/all_to_all | solution.py:79
  101.2 0.6 reshape.166
  101.8 0.7 copy.78
  102.6 0.1 reshape.145
  102.7 0.6 reshape.164
  103.4 0.7 copy.75
  104.1 0.1 reshape.144
  104.3 1.3 all-to-all-done.2
  105.6 0.6 reshape.168
  106.2 0.7 copy.83
  107.0 0.1 reshape.146
  107.1 0.2 fusion.52
  107.3 0.3 select_reduce_fusion.1
  107.7 0.1 fusion.39
  107.8 0.3 fusion.33
  108.1 0.1 collective-permute-start.1
  108.2 0.3 fusion.17
  108.5 7.0 %collective-permute-done.1 = bf16[1,64,1280]{2,1,0:T(8,128)(2,1)S(1)} collective-permute-done((bf16[1,64,1280]{2,1,0:T(8,128)(2,1)}, bf16[1,64,1280]{2,1,0:T(8,128)(2,1)S(1)}, u32[]{:S(2)}, u32[]{:S(2)}) %collective-permute-start.1) | collective-permute-done | bytes 163872 | tf_op jit(solution)/shard_map/ppermute | solution.py:101
  115.5 1.2 maximum_bitcast_fusion
  116.6 0.6 gather_fusion
  117.2 0.4 reshape_reshape_transpose.3
  117.6 0.2 copy-done.7
  117.9 0.4 fusion.22
  118.3 0.1 copy.91
  118.4 0.1 convert_element_type.32
  118.5 1.6 %reduce.5 = bf16[64,1280]{1,0:T(8,128)(2,1)S(1)} reduce(bf16[64,1,1280]{2,1,0:T(2,128)(2,1)S(1)} %bitcast.87, bf16[]{:T(256)} %broadcast.108), dimensions={1}, to_apply=%bitcast.73.reduce_sub_computation | reduce | bytes 327682
  120.1 0.7 reshape.169
  120.8 3.4 %all-to-all-start.3 = ((bf16[2,2,20480]{2,1,0:T(2,128)(2,1)}), bf16[2,2,20480]{2,1,0:T(2,128)(2,1)S(1)}, u32[]{:S(2)}, u32[]{:S(2)}) async-start(bf16[2,2,20480]{2,1,0:T(2,128)(2,1)} %reshape.169), calls=%async_computation.3 | async-start | bytes 327680 | tf_op jit(solution)/shard_map/all_to_all | solution.py:134
  124.3 4.6 %all-to-all-done.3 = bf16[2,2,20480]{2,1,0:T(2,128)(2,1)S(1)} async-done(((bf16[2,2,20480]{2,1,0:T(2,128)(2,1)}), bf16[2,2,20480]{2,1,0:T(2,128)(2,1)S(1)}, u32[]{:S(2)}, u32[]{:S(2)}) %all-to-all-start.3) | async-done | bytes 163872 | tf_op jit(solution)/shard_map/all_to_all | solution.py:134
  128.9 0.2 reshape.170
  129.1 0.7 copy.103
  129.8 2.8 %select_reduce_fusion = (f32[32,20]{0,1:T(8,128)S(1)}, f32[32,20,512]{2,0,1:T(8,128)S(1)}) fusion(pred[512]{0:T(512)(128)(4,1)S(1)} %compare_reduce_fusion, bf16[32,20,128]{2,1,0:T(8,128)(2,1)S(1)} %reshape.149, bf16[1,512,20,128]{3,1,0,2:T(8,128)(2,1)} %all-gather.3.cloned.1.call-done), kind=kOutput, calls=%fused_computation.8 | convolution fusion | flops 84868480 | bytes 4099072 | tf_op jit(solution)/shard_map/qhd,khd->qhk/dot_general | solution.py:22
  132.6 0.4 fusion.26
  133.0 0.0 all-gather.5.cloned.1.call-done
  133.0 2.3 %fusion.23 = bf16[32,20,128]{2,0,1:T(8,128)(2,1)S(1)} fusion(bf16[1,512,20,128]{3,1,0,2:T(8,128)(2,1)} %all-gather.5.cloned.1.call-done, f32[32,20,512]{2,0,1:T(8,128)S(1)} %get-tuple-element.10, f32[32,20]{0,1:T(8,128)S(1)} %get-tuple-element.9, pred[512]{0:T(512)(128)(4,1)S(1)} %compare_reduce_fusion, f32[32,20]{0,1:T(8,128)S(1)} %fusion.26), kind=kOutput, calls=%fused_computation.22 | convolution fusion | flops 85360640 | bytes 4101632 | tf_op jit(solution)/shard_map/qhk,khd->qhd/dot_general | solution.py:53
  135.4 0.1 copy.99
  135.4 0.8 reshape_broadcast_in_dim.3
  (33 shorter events, 0.3 us)
Async XLA Ops:
  7.2 122.6 %all-gather.3.cloned.1.call-start = ((), (), s32[]{:S(2)}) async-start(), calls=%async_computation.4 | async-start | bytes 3932160 | tf_op jit(solution)/shard_map/all_gather | solution.py:122
  10.3 5.2 %copy-start.3 = (bf16[1,32,2560]{2,1,0:T(8,128)(2,1)S(1)}, bf16[1,32,2560]{2,1,0:T(8,128)(2,1)}, u32[]{:S(2)}) copy-start(bf16[1,32,2560]{2,1,0:T(8,128)(2,1)} %param.9) | copy-start | bytes 491524
  10.3 97.8 %collective-permute-start = (bf16[1,64,1280]{2,1,0:T(8,128)(2,1)}, bf16[1,64,1280]{2,1,0:T(8,128)(2,1)}, u32[]{:S(2)}, u32[]{:S(2)}) collective-permute-start(bf16[1,64,1280]{2,1,0:T(8,128)(2,1)} %param.13), channel_id=1, source_target_pairs={{0,4},{4,8},{8,12},{12,0},{1,5},{5,9},{9,13},{13,1},{2,6},{6,10},{... | collective-permute-start | bytes 491528 | tf_op jit(solution)/shard_map/ppermute | solution.py:101
  13.4 95.1 %collective-permute-start.2 = (bf16[1,64,1280]{2,1,0:T(8,128)(2,1)}, bf16[1,64,1280]{2,1,0:T(8,128)(2,1)}, u32[]{:S(2)}, u32[]{:S(2)}) collective-permute-start(bf16[1,64,1280]{2,1,0:T(8,128)(2,1)} %param.13), channel_id=1, source_target_pairs={{4,0},{8,4},{12,8},{0,12},{5,1},{9,5},{13,9},{1,13},{6,2},{10,6},{... | collective-permute-start | bytes 491528 | tf_op jit(solution)/shard_map/ppermute | solution.py:104
  17.0 19.2 %copy-start = (bf16[1,512,1280]{2,1,0:T(8,128)(2,1)S(1)}, bf16[1,512,1280]{2,1,0:T(8,128)(2,1)}, u32[]{:S(2)}) copy-start(bf16[1,512,1280]{2,1,0:T(8,128)(2,1)} %param.16) | copy-start | bytes 3932164
  32.7 56.7 %all-to-all-start.1 = ((bf16[2,2,20480]{2,1,0:T(2,128)(2,1)}), bf16[2,2,20480]{2,1,0:T(2,128)(2,1)S(1)}, u32[]{:S(2)}, u32[]{:S(2)}) async-start(bf16[2,2,20480]{2,1,0:T(2,128)(2,1)} %reshape.165), calls=%async_computation.1 | async-start | bytes 327680 | tf_op jit(solution)/shard_map/all_to_all | solution.py:77
  36.2 96.9 %all-gather.5.cloned.1.call-start = ((), (), s32[]{:S(2)}) async-start(), calls=%async_computation.5 | async-start | bytes 3932160 | tf_op jit(solution)/shard_map/all_gather | solution.py:122
  38.3 0.9 copy-start.1
  38.3 1.0 copy-start.2
  38.4 17.9 %copy-start.4 = (bf16[1,32,2560]{2,1,0:T(8,128)(2,1)S(1)}, bf16[1,32,2560]{2,1,0:T(8,128)(2,1)}, u32[]{:S(2)}) copy-start(bf16[1,32,2560]{2,1,0:T(8,128)(2,1)} %param.10) | copy-start | bytes 491524
  57.2 15.7 %copy-start.5 = (bf16[1,32,2560]{2,1,0:T(8,128)(2,1)S(1)}, bf16[1,32,2560]{2,1,0:T(8,128)(2,1)}, u32[]{:S(2)}) copy-start(bf16[1,32,2560]{2,1,0:T(8,128)(2,1)} %param.11) | copy-start | bytes 491524
  89.4 8.1 %all-to-all-start = ((bf16[2,2,20480]{2,1,0:T(2,128)(2,1)}), bf16[2,2,20480]{2,1,0:T(2,128)(2,1)S(1)}, u32[]{:S(2)}, u32[]{:S(2)}) async-start(bf16[2,2,20480]{2,1,0:T(2,128)(2,1)} %reshape.163), calls=%async_computation | async-start | bytes 327680 | tf_op jit(solution)/shard_map/all_to_all | solution.py:78
  97.5 8.1 %all-to-all-start.2 = ((bf16[2,2,20480]{2,1,0:T(2,128)(2,1)}), bf16[2,2,20480]{2,1,0:T(2,128)(2,1)S(1)}, u32[]{:S(2)}, u32[]{:S(2)}) async-start(bf16[2,2,20480]{2,1,0:T(2,128)(2,1)} %reshape.167), calls=%async_computation.2 | async-start | bytes 327680 | tf_op jit(solution)/shard_map/all_to_all | solution.py:79
  101.2 6.6 %copy-start.6 = (pred[256]{0:T(512)(128)(4,1)}, pred[256]{0:T(512)(128)(4,1)S(1)}, u32[]{:S(2)}) copy-start(pred[256]{0:T(512)(128)(4,1)S(1)} %compare_or_fusion) | copy-start | bytes 772
  108.1 7.4 %collective-permute-start.1 = (bf16[1,64,1280]{2,1,0:T(8,128)(2,1)}, bf16[1,64,1280]{2,1,0:T(8,128)(2,1)S(1)}, u32[]{:S(2)}, u32[]{:S(2)}) collective-permute-start(bf16[1,64,1280]{2,1,0:T(8,128)(2,1)} %collective-permute-done), channel_id=1, source_target_pairs={{0,4},{4,8},{8,12},{12,0},{1,5},{5,9},{9,13},{13,1},{2,6},{6,10},{... | collective-permute-start | bytes 491528 | tf_op jit(solution)/shard_map/ppermute | solution.py:101
  117.2 0.7 copy-start.7
  118.3 6.0 %copy-start.8 = (s32[1,512]{1,0:T(1,128)S(1)}, s32[1,512]{1,0:T(1,128)}, u32[]{:S(2)}) copy-start(s32[1,512]{1,0:T(1,128)} %param.17) | copy-start | bytes 6148
  120.8 8.1 %all-to-all-start.3 = ((bf16[2,2,20480]{2,1,0:T(2,128)(2,1)}), bf16[2,2,20480]{2,1,0:T(2,128)(2,1)S(1)}, u32[]{:S(2)}, u32[]{:S(2)}) async-start(bf16[2,2,20480]{2,1,0:T(2,128)(2,1)} %reshape.169), calls=%async_computation.3 | async-start | bytes 327680 | tf_op jit(solution)/shard_map/all_to_all | solution.py:134
Sparse Core Ops, SparseCore 0:
  10.4 43.4 all-gather.2
  55.5 39.8 all-gather.4
